TPU v7x, 32 devices: a whole 2x2x4 slice. The times are simulated.
32 devices in a mesh: seq: 8 (over y, x, core), tp: 4 (over z).
Axes of the slice: x: 2, y: 2, z: 4, core: 2. Of those that a mesh axis runs over, the one named last changes fastest.
Arguments:
- tokens: bfloat16 [128, 17, 1152], P('seq'), may hold values from -6 to 6
- cotangent: bfloat16 [128, 17, 1152], P('seq'), may hold values from -6 to 6
- caption: bfloat16 [4, 300, 1152], replicated, may hold values from -6 to 6
- condition: float32 [4, 1152], replicated, may hold values from -6 to 6
- frames: int32 [4], replicated, may hold values from 1 to 17, 44 in all
- cap_len: int32 [4], replicated, may hold values from 1 to 300, 600 in all
- clip_of: int32 [128], P('seq'), may hold values from 0 to 3
- w_qkv: bfloat16 [1152, 3, 1152], P('seq', None, 'tp'), may hold values from -0.1875 to 0.1875
- w_out: bfloat16 [1152, 1152], P('tp', 'seq'), may hold values from -0.375 to 0.375
- w_query2: bfloat16 [1152, 1152], P('seq', 'tp'), may hold values from -0.1875 to 0.1875
- w_kv2: bfloat16 [1152, 2, 1152], P('seq', None, 'tp'), may hold values from -0.1875 to 0.1875
- w_out2: bfloat16 [1152, 1152], P('tp', 'seq'), may hold values from -0.75 to 0.75
- w_up: bfloat16 [1152, 4608], P('seq', 'tp'), may hold values from -0.1875 to 0.1875
- w_down: bfloat16 [4608, 1152], P('tp', 'seq'), may hold values from -0.09375 to 0.09375
- w_ada: bfloat16 [1152, 6912], P('seq', 'tp'), may hold values from -0.1875 to 0.1875
Outputs:
- output: bfloat16 [128, 17, 1152], P('seq')
- d_tokens: bfloat16 [128, 17, 1152], P('seq')
- d_caption: float32 [4, 300, 1152], P(None, None, 'tp')
- d_condition: float32 [4, 1152], replicated
- d_w_qkv: float32 [1152, 3, 1152], P('seq', None, 'tp')
- d_w_out: float32 [1152, 1152], P('tp', 'seq')
- d_w_query2: float32 [1152, 1152], P('seq', 'tp')
- d_w_kv2: float32 [1152, 2, 1152], P('seq', None, 'tp')
- d_w_out2: float32 [1152, 1152], P('tp', 'seq')
- d_w_up: float32 [1152, 4608], P('seq', 'tp')
- d_w_down: float32 [4608, 1152], P('tp', 'seq')
- d_w_ada: float32 [1152, 6912], P('seq', 'tp')
Inputs may be any that keep to these rules, and one draw needn't show every extreme that they name: frames of each clip; they add up to 44 and one clip has 17. `cap_len`: live caption tokens of each clip, the first ones of its slots; they add up to 600 and one clip has 300.
All inputs are finite; a program needn't handle non-finite values.
Results may differ from a plain program's by a relative error of at most 0.024.
Values may be sent and summed in bfloat16 or wider, within the bound.
No kernel may reach another device: no remote copies, remote signals or barrier semaphores. Data moves between devices by JAX's collectives and lax.ppermute only.
A program may use at most 128 MiB of HBM per device.

v0:
```python
import jax
import jax.numpy as jnp
from jax import lax
from jax.sharding import PartitionSpec as P

HDIM = 72
CLIPS = 4
EPSILON = 1e-06
NEG_FILL = -1e30
HIGHEST = lax.Precision.HIGHEST


def normalize(rows):
    center = rows - jnp.mean(rows, -1, keepdims=True)
    return center * lax.rsqrt(jnp.mean(center * center, -1, keepdims=True) + EPSILON)


def modulate(rows, shift, scale):
    return normalize(rows) * (1.0 + scale[:, None, :]) + shift[:, None, :]


def total_rows(partial_value):
    return lax.psum(partial_value, "tp")


def frame_attention(triple, live, head_scale):
    raw = (
        jnp.einsum(
            "lfhe,lghe->lhfg", triple[:, :, 0], triple[:, :, 1], preferred_element_type=jnp.float32
        )
        * head_scale
    )
    probs = jax.nn.softmax(jnp.where(live[:, None, None, :], raw, NEG_FILL), axis=-1)
    result = jnp.einsum(
        "lhfg,lghe->lfhe",
        probs.astype(jnp.bfloat16),
        triple[:, :, 2],
        preferred_element_type=jnp.float32,
    )
    return (probs, result.astype(jnp.bfloat16))


def cross_scores(query, keys, clips, key_clip, key_live, head_scale):
    raw = jnp.einsum("rhe,khe->hrk", query, keys, preferred_element_type=jnp.float32) * head_scale
    allowed = (clips[:, None] == key_clip[None, :]) & key_live[None, :]
    return jnp.where(allowed[None], raw, NEG_FILL)


def shards(
    tokens,
    cotangent,
    caption,
    condition,
    frames,
    cap_len,
    clip_of,
    w_qkv,
    w_out,
    w_query2,
    w_kv2,
    w_out2,
    w_up,
    w_down,
    w_ada,
):
    seqs, fmax, width = tokens.shape
    row_count = seqs * fmax
    inner = w_qkv.shape[2]
    local_heads = inner // HDIM
    head_scale = HDIM ** (-0.5)
    full_qkv, full_out, full_query2, full_kv2, full_out2, full_up, full_down, full_ada = (
        lax.all_gather(w_qkv, "seq", axis=0, tiled=True),
        lax.all_gather(w_out, "seq", axis=1, tiled=True),
        lax.all_gather(w_query2, "seq", axis=0, tiled=True),
        lax.all_gather(w_kv2, "seq", axis=0, tiled=True),
        lax.all_gather(w_out2, "seq", axis=1, tiled=True),
        lax.all_gather(w_up, "seq", axis=0, tiled=True),
        lax.all_gather(w_down, "seq", axis=1, tiled=True),
        lax.all_gather(w_ada, "seq", axis=0, tiled=True),
    )
    qkv_matrix = full_qkv.reshape(width, 3 * inner)
    kv_matrix = full_kv2.reshape(width, 2 * inner)
    scaled = jax.nn.silu(condition).astype(jnp.bfloat16)
    mod_part = jnp.dot(scaled, full_ada, preferred_element_type=jnp.float32)
    mods = lax.all_gather(mod_part, "tp", axis=1, tiled=True).reshape(CLIPS, 6, width)
    clip_ids = jnp.arange(CLIPS)
    clip_hot = clip_of[:, None] == clip_ids[None, :]
    seq_mods = jnp.sum(jnp.where(clip_hot[:, :, None, None], mods[None], 0.0), 1)
    seq_frames = jnp.sum(jnp.where(clip_hot, frames[None, :], 0), 1)
    live = jnp.arange(fmax)[None, :] < seq_frames[:, None]
    own_live = live.astype(jnp.float32)[:, :, None]
    own_hot = clip_hot.astype(jnp.float32)
    key_count = caption.shape[0] * caption.shape[1]
    key_clip = jnp.arange(key_count) // caption.shape[1]
    key_len = jnp.sum(jnp.where(key_clip[:, None] == clip_ids[None, :], cap_len[None, :], 0), 1)
    key_live = jnp.arange(key_count) % caption.shape[1] < key_len
    row_clip = jnp.repeat(clip_of, fmax)
    block_seqs = min(32, seqs)
    blocks = seqs // block_seqs
    block_rows = block_seqs * fmax
    block_clip = row_clip.reshape(blocks, block_rows)
    own_input = tokens.astype(jnp.float32)
    attn_in = (
        modulate(own_input, seq_mods[:, 0], seq_mods[:, 1])
        .astype(jnp.bfloat16)
        .reshape(row_count, width)
    )
    triple = (
        jnp.dot(attn_in, qkv_matrix, preferred_element_type=jnp.float32)
        .astype(jnp.bfloat16)
        .reshape(seqs, fmax, 3, local_heads, HDIM)
    )
    probs, frame_out = frame_attention(triple, live, head_scale)
    frame_out = frame_out.reshape(row_count, inner)
    branch_one = total_rows(
        jnp.dot(frame_out, full_out, preferred_element_type=jnp.float32).reshape(seqs, fmax, width)
    )
    first = own_input + seq_mods[:, 2][:, None, :] * branch_one
    first_low = first.astype(jnp.bfloat16).reshape(row_count, width)
    cross_query = (
        jnp.dot(first_low, full_query2, preferred_element_type=jnp.float32)
        .astype(jnp.bfloat16)
        .reshape(blocks, block_rows, local_heads, HDIM)
    )
    cross_kv = (
        jnp.dot(caption.reshape(key_count, width), kv_matrix, preferred_element_type=jnp.float32)
        .astype(jnp.bfloat16)
        .reshape(key_count, 2, local_heads, HDIM)
    )
    cross_key = cross_kv[:, 0]
    cross_value = cross_kv[:, 1]

    def cross_block(pair):
        query, clips = pair
        scores = cross_scores(query, cross_key, clips, key_clip, key_live, head_scale)
        top = jnp.max(scores, -1, keepdims=True)
        weights = jnp.exp(scores - top)
        denom = jnp.sum(weights, -1, keepdims=True)
        block_out = jnp.einsum(
            "hrk,khe->rhe",
            (weights / denom).astype(jnp.bfloat16),
            cross_value,
            preferred_element_type=jnp.float32,
        )
        return (block_out.astype(jnp.bfloat16), (top + jnp.log(denom))[..., 0])

    cross_out, cross_lse = lax.map(cross_block, (cross_query, block_clip))
    cross_out = cross_out.reshape(row_count, inner)
    second = first + total_rows(
        jnp.dot(cross_out, full_out2, preferred_element_type=jnp.float32).reshape(seqs, fmax, width)
    )
    mlp_in = (
        modulate(second, seq_mods[:, 3], seq_mods[:, 4])
        .astype(jnp.bfloat16)
        .reshape(row_count, width)
    )
    hidden_pre = jnp.dot(mlp_in, full_up, preferred_element_type=jnp.float32)
    hidden = jax.nn.gelu(hidden_pre, approximate=True).astype(jnp.bfloat16)
    branch_three = total_rows(
        jnp.dot(hidden, full_down, preferred_element_type=jnp.float32).reshape(seqs, fmax, width)
    )
    third = second + seq_mods[:, 5][:, None, :] * branch_three
    output = (third * own_live).astype(jnp.bfloat16)
    grad_three = cotangent.astype(jnp.float32) * own_live
    d_branch3 = (
        (seq_mods[:, 5][:, None, :] * grad_three).astype(jnp.bfloat16).reshape(row_count, width)
    )
    grad_down = jnp.einsum("rk,rd->kd", hidden, d_branch3, preferred_element_type=jnp.float32)
    d_hidden = jnp.einsum("rd,kd->rk", d_branch3, full_down, preferred_element_type=jnp.float32)
    gelu_pull = jax.vjp(lambda value: jax.nn.gelu(value, approximate=True), hidden_pre)[1]
    d_pre = gelu_pull(d_hidden)[0].astype(jnp.bfloat16)
    grad_up = jnp.einsum("rd,rk->dk", mlp_in, d_pre, preferred_element_type=jnp.float32)
    d_mlp = total_rows(
        jnp.einsum("rk,dk->rd", d_pre, full_up, preferred_element_type=jnp.float32).reshape(
            seqs, fmax, width
        )
    )
    second_pull = jax.vjp(modulate, second, seq_mods[:, 3], seq_mods[:, 4])[1]
    norm_two, d_shift2, d_scale2 = second_pull(d_mlp)
    grad_two = grad_three + norm_two
    d_branch2 = grad_two.astype(jnp.bfloat16).reshape(row_count, width)
    grad_out2 = jnp.einsum("rc,rd->cd", cross_out, d_branch2, preferred_element_type=jnp.float32)
    d_cross = (
        jnp.einsum("rd,cd->rc", d_branch2, full_out2, preferred_element_type=jnp.float32)
        .astype(jnp.bfloat16)
        .reshape(blocks, block_rows, local_heads, HDIM)
    )

    def cross_back(carry, item):
        key_sum, value_sum = carry
        query, clips, block_lse, grad_block = item
        scores = cross_scores(query, cross_key, clips, key_clip, key_live, head_scale)
        weights = jnp.exp(scores - block_lse[..., None])
        value_sum = value_sum + jnp.einsum(
            "hrk,rhe->khe",
            weights.astype(jnp.bfloat16),
            grad_block,
            preferred_element_type=jnp.float32,
        )
        grad_weights = jnp.einsum(
            "rhe,khe->hrk", grad_block, cross_value, preferred_element_type=jnp.float32
        )
        grad_scores = (
            weights * (grad_weights - jnp.sum(weights * grad_weights, -1, keepdims=True))
        ).astype(jnp.bfloat16)
        grad_query = (
            jnp.einsum("hrk,khe->rhe", grad_scores, cross_key, preferred_element_type=jnp.float32)
            * head_scale
        ).astype(jnp.bfloat16)
        key_sum = (
            key_sum
            + jnp.einsum("hrk,rhe->khe", grad_scores, query, preferred_element_type=jnp.float32)
            * head_scale
        )
        return ((key_sum, value_sum), grad_query)

    zero_keys = jnp.zeros((key_count, local_heads, HDIM), jnp.float32)
    (key_grad, value_grad), d_query = lax.scan(
        cross_back, (zero_keys, zero_keys), (cross_query, block_clip, cross_lse, d_cross)
    )
    d_query = d_query.reshape(row_count, inner)
    grad_query2 = jnp.einsum("rd,rc->dc", first_low, d_query, preferred_element_type=jnp.float32)
    grad_one = grad_two + total_rows(
        jnp.einsum("rc,dc->rd", d_query, full_query2, preferred_element_type=jnp.float32).reshape(
            seqs, fmax, width
        )
    )
    d_branch1 = (
        (seq_mods[:, 2][:, None, :] * grad_one).astype(jnp.bfloat16).reshape(row_count, width)
    )
    grad_out = jnp.einsum("rc,rd->cd", frame_out, d_branch1, preferred_element_type=jnp.float32)
    d_frame = (
        jnp.einsum("rd,cd->rc", d_branch1, full_out, preferred_element_type=jnp.float32)
        .astype(jnp.bfloat16)
        .reshape(seqs, fmax, local_heads, HDIM)
    )
    d_value = jnp.einsum(
        "lhfg,lfhe->lghe", probs.astype(jnp.bfloat16), d_frame, preferred_element_type=jnp.float32
    )
    d_probs = jnp.einsum(
        "lfhe,lghe->lhfg", d_frame, triple[:, :, 2], preferred_element_type=jnp.float32
    )
    d_scores = (probs * (d_probs - jnp.sum(probs * d_probs, -1, keepdims=True))).astype(
        jnp.bfloat16
    )
    d_queries = (
        jnp.einsum("lhfg,lghe->lfhe", d_scores, triple[:, :, 1], preferred_element_type=jnp.float32)
        * head_scale
    )
    d_keys = (
        jnp.einsum("lhfg,lfhe->lghe", d_scores, triple[:, :, 0], preferred_element_type=jnp.float32)
        * head_scale
    )
    d_triple = (
        jnp.stack([d_queries, d_keys, d_value], 2)
        .astype(jnp.bfloat16)
        .reshape(row_count, 3 * inner)
    )
    grad_qkv = jnp.einsum(
        "rd,rc->dc", attn_in, d_triple, preferred_element_type=jnp.float32
    ).reshape(width, 3, inner)
    d_attn = total_rows(
        jnp.einsum("rc,dc->rd", d_triple, qkv_matrix, preferred_element_type=jnp.float32).reshape(
            seqs, fmax, width
        )
    )
    first_pull = jax.vjp(modulate, own_input, seq_mods[:, 0], seq_mods[:, 1])[1]
    norm_one, d_shift1, d_scale1 = first_pull(d_attn)
    d_tokens = (grad_one + norm_one).astype(jnp.bfloat16)
    d_gate1 = jnp.sum(grad_one * branch_one, 1)
    d_gate2 = jnp.sum(grad_three * branch_three, 1)
    seq_terms = jnp.stack([d_shift1, d_scale1, d_gate1, d_shift2, d_scale2, d_gate2], 1)
    d_mods = jnp.einsum("lc,ljd->cjd", own_hot, seq_terms, precision=HIGHEST).reshape(
        CLIPS, 6 * width
    )
    kv_grad = jnp.stack([key_grad, value_grad], 1)
    kv_total, mods_total = (
        lax.psum(kv_grad.astype(jnp.bfloat16), "seq").astype(jnp.float32),
        lax.psum(d_mods.astype(jnp.bfloat16), "seq").astype(jnp.float32),
    )
    col_count = mods_total.shape[1] // lax.axis_size("tp")
    mod_cols = lax.dynamic_slice_in_dim(mods_total, lax.axis_index("tp") * col_count, col_count, 1)
    seq_rows = w_ada.shape[0]
    seq_start = lax.axis_index("seq") * seq_rows
    scaled_rows = lax.dynamic_slice_in_dim(scaled, seq_start, seq_rows, 1).astype(jnp.float32)
    grad_ada = jnp.einsum("cd,ck->dk", scaled_rows, mod_cols, precision=HIGHEST)
    silu_pull = jax.vjp(jax.nn.silu, condition)[1]
    cond_part = silu_pull(
        jnp.einsum("ck,dk->cd", mod_cols, full_ada.astype(jnp.float32), precision=HIGHEST)
    )[0]
    d_condition = lax.psum(cond_part, "tp")
    kv_low = kv_total.astype(jnp.bfloat16).reshape(key_count, 2 * inner)
    caption_rows = lax.dynamic_slice_in_dim(
        caption.reshape(key_count, width), seq_start, seq_rows, 1
    )
    grad_kv2 = jnp.einsum(
        "kd,kc->dc", caption_rows, kv_low, preferred_element_type=jnp.float32
    ).reshape(seq_rows, 2, inner)
    caption_part = jnp.einsum(
        "kc,dc->kd", kv_low, kv_matrix, preferred_element_type=jnp.float32
    ).reshape(caption.shape)
    d_caption = lax.psum_scatter(
        caption_part.astype(jnp.bfloat16), "tp", scatter_dimension=2, tiled=True
    ).astype(jnp.float32)
    summed = (
        lax.psum_scatter(
            grad_qkv.astype(jnp.bfloat16), "seq", scatter_dimension=0, tiled=True
        ).astype(jnp.float32),
        lax.psum_scatter(
            grad_out.astype(jnp.bfloat16), "seq", scatter_dimension=1, tiled=True
        ).astype(jnp.float32),
        lax.psum_scatter(
            grad_query2.astype(jnp.bfloat16), "seq", scatter_dimension=0, tiled=True
        ).astype(jnp.float32),
        lax.psum_scatter(
            grad_out2.astype(jnp.bfloat16), "seq", scatter_dimension=1, tiled=True
        ).astype(jnp.float32),
        lax.psum_scatter(
            grad_up.astype(jnp.bfloat16), "seq", scatter_dimension=0, tiled=True
        ).astype(jnp.float32),
        lax.psum_scatter(
            grad_down.astype(jnp.bfloat16), "seq", scatter_dimension=1, tiled=True
        ).astype(jnp.float32),
    )
    return (
        output,
        d_tokens,
        d_caption,
        d_condition,
        summed[0],
        summed[1],
        summed[2],
        grad_kv2,
        summed[3],
        summed[4],
        summed[5],
        grad_ada,
    )


def solution(mesh):
    return jax.shard_map(
        shards,
        mesh=mesh,
        in_specs=(
            P("seq", None, None),
            P("seq", None, None),
            P(),
            P(),
            P(),
            P(),
            P("seq"),
            P("seq", None, "tp"),
            P("tp", "seq"),
            P("seq", "tp"),
            P("seq", None, "tp"),
            P("tp", "seq"),
            P("seq", "tp"),
            P("tp", "seq"),
            P("seq", "tp"),
        ),
        out_specs=(
            P("seq", None, None),
            P("seq", None, None),
            P(None, None, "tp"),
            P(),
            P("seq", None, "tp"),
            P("tp", "seq"),
            P("seq", "tp"),
            P("seq", None, "tp"),
            P("tp", "seq"),
            P("seq", "tp"),
            P("tp", "seq"),
            P("seq", "tp"),
        ),
        check_vma=False,
    )
```

profile of v0, /device:TPU:0, one launch (start us, length us, event | category | flops | bytes accessed | tf_op | source)
XLA Modules:
  0.0 1068.3 jit_solution(13612882484881826433)
XLA Ops:
  14.8 15.0 %all_gather.30 = bf16[288,1152]{0,1:T(8,128)(2,1)S(1)} all-gather(bf16[288,144]{0,1:T(8,128)(2,1)S(1)} %copy-done.45), channel_id=1, replica_groups=mesh['seq'=8,'tp'=4] {'seq'}, dimensions={1}, use_global_device_ids=true | all-gather | bytes 746496 | tf_op jit(solution)/shard_map/all_gather | solution.py:73
  29.7 13.7 %all_gather.32 = bf16[1152,288]{1,0:T(8,128)(2,1)S(1)} all-gather(bf16[144,288]{1,0:T(8,128)(2,1)S(1)} %copy-done.46), channel_id=1, replica_groups=mesh['seq'=8,'tp'=4] {'seq'}, dimensions={0}, use_global_device_ids=true | all-gather | bytes 746496 | tf_op jit(solution)/shard_map/all_gather | solution.py:74
  43.4 11.3 %all_gather.33 = bf16[288,1152]{0,1:T(8,128)(2,1)} all-gather(bf16[288,144]{0,1:T(8,128)(2,1)S(1)} %copy-done.47), channel_id=1, replica_groups=mesh['seq'=8,'tp'=4] {'seq'}, dimensions={1}, use_global_device_ids=true | all-gather | bytes 746496 | tf_op jit(solution)/shard_map/all_gather | solution.py:76
  56.6 3.3 reshape.348
  59.9 4.3 copy.144
  64.2 21.8 %all-gather.7.cloned.1.call-done = bf16[1152,1728]{1,0:T(8,128)(2,1)} async-done(((bf16[144,1728]{1,0:T(8,128)(2,1)}), bf16[1152,1728]{1,0:T(8,128)(2,1)}) %all-gather.7.cloned.1.call-update) | async-done | bytes 3981328 | tf_op jit(solution)/shard_map/all_gather | solution.py:79
  86.0 2.8 convolution_bitcast_fusion
  88.8 13.4 %all-gather = f32[4,1728,4]{1,2,0:T(4,128)S(1)} all-gather(f32[1,1728,4]{1,2,0:T(4,128)S(1)} %convolution_bitcast_fusion), channel_id=1, replica_groups=mesh['seq'=8,'tp'=4] {'tp'}, dimensions={0}, use_global_device_ids=true | all-gather | bytes 138240 | tf_op jit(solution)/shard_map/all_gather | solution.py:85
  105.5 3.5 convolution_convert_fusion.9
  109.0 2.9 reshape.347
  115.8 2.7 fusion.37
  123.3 5.6 copy.152
  128.9 5.6 convolution_convert_fusion.4
  134.5 63.4 %all-reduce.8.cloned.1.call-done = f32[16,17,1152]{2,1,0:T(8,128)} async-done(((f32[16,17,1152]{2,1,0:T(8,128)}), f32[16,17,1152]{2,1,0:T(8,128)}) %all-reduce.8.cloned.1.call-update) | async-done | bytes 1253392 | tf_op jit(solution)/shard_map/psum | solution.py:23
  201.1 2.5 fusion.98
  212.2 73.3 %all-reduce.10.cloned.1.call-done = f32[16,17,1152]{2,1,0:T(8,128)} async-done(((f32[16,17,1152]{2,1,0:T(8,128)}), f32[16,17,1152]{2,1,0:T(8,128)}) %all-reduce.10.cloned.1.call-update) | async-done | bytes 1253392 | tf_op jit(solution)/shard_map/psum | solution.py:23
  285.5 2.5 fusion.94
  291.0 2.2 reshape.354
  293.2 2.3 reshape.352
  295.4 21.2 %all-gather.15.cloned.1.call-done = bf16[1152,1152]{0,1:T(8,128)(2,1)} async-done(((bf16[1152,144]{0,1:T(8,128)(2,1)}), bf16[1152,1152]{0,1:T(8,128)(2,1)}) %all-gather.15.cloned.1.call-update) | async-done | bytes 2654224 | tf_op jit(solution)/shard_map/all_gather | solution.py:78
  316.6 4.1 fusion.99
  320.7 28.1 %all-gather.13.cloned.1.call-done = bf16[1152,1152]{1,0:T(8,128)(2,1)} async-done(((bf16[144,1152]{1,0:T(8,128)(2,1)}), bf16[1152,1152]{1,0:T(8,128)(2,1)}) %all-gather.13.cloned.1.call-update) | async-done | bytes 2654224 | tf_op jit(solution)/shard_map/all_gather | solution.py:77
  348.8 5.0 fusion.36
  354.6 2.2 fusion.100
  356.8 2.7 reshape.355
  359.8 75.4 %all-reduce.12.cloned.1.call-done = f32[16,17,1152]{2,1,0:T(8,128)} async-done(((f32[16,17,1152]{2,1,0:T(8,128)}), f32[16,17,1152]{2,1,0:T(8,128)}) %all-reduce.12.cloned.1.call-update) | async-done | bytes 1253392 | tf_op jit(solution)/shard_map/psum | solution.py:23
  435.2 3.3 multiply_reduce_fusion.2
  441.6 2.2 reshape.356
  443.8 2.6 convolution_convert_fusion.12
  447.5 4.6 multiply_reduce_fusion
  458.0 3.1 fusion.44
  461.2 2.7 fusion.15
  463.9 4.0 fusion.16
  469.2 2.9 convolution_convert_fusion.5
  473.1 2.8 convolution_convert_fusion.6
  476.0 59.8 %all-reduce.14.cloned.1.call-done = f32[16,17,1152]{2,1,0:T(8,128)} async-done(((f32[16,17,1152]{2,1,0:T(8,128)}), f32[16,17,1152]{2,1,0:T(8,128)}) %all-reduce.14.cloned.1.call-update) | async-done | bytes 1253392 | tf_op jit(solution)/shard_map/psum | solution.py:23
  535.8 3.9 multiply_reduce_fusion.3
  542.0 2.2 reshape.357
  544.2 2.7 convolution_convert_fusion.7
  547.4 4.5 convolution_convert_fusion.1
  552.0 4.7 convolution_convert_fusion
  556.8 4.5 fusion.91
  561.3 2.7 reshape.353
  574.7 2.9 reshape.378
  577.6 4.3 fusion.101
  582.1 2.2 reshape.375
  587.4 4.5 convolution_convert_fusion.3
  591.9 4.7 all-reduce.16.cloned.1.call-done
  596.6 2.6 fusion.52
  600.2 4.2 dot_general.164
  604.5 6.6 convolution_convert_fusion.2
  611.1 23.5 %reduce-scatter.16.cloned.1.call-done = bf16[288,144]{0,1:T(8,128)(2,1)} async-done(((bf16[288,1152]{0,1:T(8,128)(2,1)}), bf16[288,144]{0,1:T(8,128)(2,1)}) %reduce-scatter.16.cloned.1.call-update) | async-done | bytes 82960 | tf_op jit(solution)/shard_map/reduce_scatter | solution.py:315
  636.2 36.7 %reduce-scatter.14.cloned.1.call-done = bf16[144,288]{1,0:T(8,128)(2,1)} async-done(((bf16[1152,288]{1,0:T(8,128)(2,1)}), bf16[144,288]{1,0:T(8,128)(2,1)}) %reduce-scatter.14.cloned.1.call-update) | async-done | bytes 82960 | tf_op jit(solution)/shard_map/reduce_scatter | solution.py:312
  674.4 37.7 %reduce-scatter.12.cloned.1.call-done = bf16[288,144]{0,1:T(8,128)(2,1)} async-done(((bf16[288,1152]{0,1:T(8,128)(2,1)}), bf16[288,144]{0,1:T(8,128)(2,1)}) %reduce-scatter.12.cloned.1.call-update) | async-done | bytes 82960 | tf_op jit(solution)/shard_map/reduce_scatter | solution.py:309
  713.7 45.6 %reduce-scatter.18.cloned.1.call-done = bf16[144,1152]{1,0:T(8,128)(2,1)} async-done(((bf16[1152,1152]{1,0:T(8,128)(2,1)}), bf16[144,1152]{1,0:T(8,128)(2,1)}) %reduce-scatter.18.cloned.1.call-update) | async-done | bytes 331792 | tf_op jit(solution)/shard_map/reduce_scatter | solution.py:318
  761.2 45.7 %reduce-scatter.20.cloned.1.call-done = bf16[1152,144]{0,1:T(8,128)(2,1)} async-done(((bf16[1152,1152]{0,1:T(8,128)(2,1)}), bf16[1152,144]{0,1:T(8,128)(2,1)}) %reduce-scatter.20.cloned.1.call-update) | async-done | bytes 331792 | tf_op jit(solution)/shard_map/reduce_scatter | solution.py:321
  808.7 135.2 %all-reduce.18.cloned.1.call-done = (f32[16,17,1152]{2,1,0:T(8,128)}, f32[16,17,1152]{2,1,0:T(8,128)}) async-done(((f32[16,17,1152]{2,1,0:T(8,128)}, f32[16,17,1152]{2,1,0:T(8,128)}), (f32[16,17,1152]{2,1,0:T(8,128)}, f32[16,17,1152]{2,1,0:T(8,128)})) %all-reduce.18.cloned.1.call-update) | async-done | bytes 2506768 | tf_op jit(solution)/shard_map/psum | solution.py:23
  943.9 2.1 fusion.25
  951.2 24.9 %psum.70 = bf16[4,6912]{1,0:T(4,128)(2,1)S(1)} all-reduce(bf16[4,6912]{1,0:T(4,128)(2,1)S(1)} %bitcast.198), channel_id=1, replica_groups=mesh['seq'=8,'tp'=4] {'seq'}, use_global_device_ids=true, to_apply=%region_31.32 | all-reduce | flops 27648 | bytes 110592 | tf_op jit(solution)/shard_map/psum | solution.py:279
  976.1 3.4 fusion.68
  979.5 17.6 %psum.71 = f32[4,1152]{1,0:T(4,128)} all-reduce(f32[4,1152]{1,0:T(4,128)S(1)} %fusion.68), channel_id=1, replica_groups=mesh['seq'=8,'tp'=4] {'tp'}, use_global_device_ids=true, to_apply=%region_32.33 | all-reduce | flops 4608 | bytes 36864 | tf_op jit(solution)/shard_map/psum | solution.py:291
  997.1 2.0 fusion.73
  1001.1 57.7 %reduce-scatter.8.cloned.1.call-done = bf16[4,300,288]{1,2,0:T(8,128)(2,1)} async-done(((bf16[4,300,1152]{1,2,0:T(8,128)(2,1)}), bf16[4,300,288]{1,2,0:T(8,128)(2,1)}) %reduce-scatter.8.cloned.1.call-update) | async-done | bytes 691216 | tf_op jit(solution)/shard_map/reduce_scatter | solution.py:302
  1058.8 2.5 convert_element_type.205
  (261 shorter events, 82.6 us)
Async XLA Ops:
  7.2 6.5 copy-start.1
  7.2 7.5 copy-start.48
  7.2 7.6 copy-start.45
  7.2 22.5 %copy-start.46 = (bf16[144,288]{1,0:T(8,128)(2,1)S(1)}, bf16[144,288]{1,0:T(8,128)(2,1)}, u32[]{:S(2)}) copy-start(bf16[144,288]{1,0:T(8,128)(2,1)} %param.24) | copy-start | bytes 248836
  7.2 52.7 %all-gather.9.cloned.1.call-start = ((), (), s32[]{:S(2)}) async-start(), calls=%async_computation.8 | async-start | bytes 2985984 | tf_op jit(solution)/shard_map/all_gather | solution.py:72
  8.0 78.0 %all-gather.7.cloned.1.call-start = ((), (), s32[]{:S(2)}) async-start(), calls=%async_computation.7 | async-start | bytes 4644864 | tf_op jit(solution)/shard_map/all_gather | solution.py:79
  8.7 34.7 %copy-start.47 = (bf16[288,144]{0,1:T(8,128)(2,1)S(1)}, bf16[288,144]{0,1:T(8,128)(2,1)}, u32[]{:S(2)}) copy-start(bf16[288,144]{0,1:T(8,128)(2,1)} %param.26) | copy-start | bytes 248836
  8.7 114.6 %all-gather.11.cloned.1.call-start = ((), (), s32[]{:S(2)}) async-start(), calls=%async_computation.10 | async-start | bytes 1990656 | tf_op jit(solution)/shard_map/all_gather | solution.py:75
  9.5 188.4 %all-reduce.8.cloned.1.call-start = ((), (), s32[]{:S(2)}) async-start(), calls=%async_computation.9 | async-start | bytes 3538944 | tf_op jit(solution)/shard_map/psum | solution.py:23
  13.6 41.1 %copy-start.17 = (bf16[4,300,1152]{2,0,1:T(4,128)(2,1)S(1)}, bf16[4,300,1152]{2,0,1:T(4,128)(2,1)}, u32[]{:S(2)}) copy-start(bf16[4,300,1152]{2,0,1:T(4,128)(2,1)} %param.17) | copy-start | bytes 8294404
  14.7 71.3 %copy-start.56 = (bf16[4,1152]{1,0:T(4,128)(2,1)}, bf16[4,1152]{1,0:T(4,128)(2,1)S(1)}, u32[]{:S(2)}) copy-start(bf16[4,1152]{1,0:T(4,128)(2,1)S(1)} %multiply_convert_fusion.6) | copy-start | bytes 27652
  29.7 90.2 %copy-start.9 = (bf16[288,1152]{0,1:T(8,128)(2,1)}, bf16[288,1152]{0,1:T(8,128)(2,1)S(1)}, u32[]{:S(2)}) copy-start(bf16[288,1152]{0,1:T(8,128)(2,1)S(1)} %all_gather.30) | copy-start | bytes 1990660
  43.4 156.5 %copy-start.10 = (bf16[1152,288]{1,0:T(8,128)(2,1)}, bf16[1152,288]{1,0:T(8,128)(2,1)S(1)}, u32[]{:S(2)}) copy-start(bf16[1152,288]{1,0:T(8,128)(2,1)S(1)} %all_gather.32) | copy-start | bytes 1990660
  103.3 182.3 %copy-start.31 = (f32[16,1152]{1,0:T(8,128)}, f32[16,1152]{1,0:T(8,128)S(1)}, u32[]{:S(2)}) copy-start(f32[16,1152]{1,0:T(8,128)S(1)} %get-tuple-element.159) | copy-start | bytes 221188
  103.3 185.1 %copy-start.36 = (f32[16,1152]{1,0:T(8,128)}, f32[16,1152]{1,0:T(8,128)S(1)}, u32[]{:S(2)}) copy-start(f32[16,1152]{1,0:T(8,128)S(1)} %get-tuple-element.154) | copy-start | bytes 221188
  104.4 4.6 copy-start.8
  113.3 2.4 copy-start.25
  113.3 5.2 copy-start.27
  113.3 5.2 copy-start.42
  115.7 2.7 copy-start.43
  119.6 2.3 copy-start.18
  120.0 2.2 copy-start.61
  120.0 2.3 copy-start.59
  121.9 163.6 %all-reduce.10.cloned.1.call-start = ((), (), s32[]{:S(2)}) async-start(), calls=%async_computation.11 | async-start | bytes 3538944 | tf_op jit(solution)/shard_map/psum | solution.py:23
  128.9 5.6 copy-start.30
  199.8 3.8 copy-start.13
  203.6 2.4 copy-start
  203.6 2.4 copy-start.54
  203.6 2.5 copy-start.14
  206.1 2.8 copy-start.11
  210.8 105.8 %all-gather.15.cloned.1.call-start = ((), (), s32[]{:S(2)}) async-start(), calls=%async_computation.13 | async-start | bytes 2985984 | tf_op jit(solution)/shard_map/all_gather | solution.py:78
  211.4 137.4 %all-gather.13.cloned.1.call-start = ((), (), s32[]{:S(2)}) async-start(), calls=%async_computation.12 | async-start | bytes 2985984 | tf_op jit(solution)/shard_map/all_gather | solution.py:77
  212.2 223.0 %all-reduce.12.cloned.1.call-start = ((), (), s32[]{:S(2)}) async-start(), calls=%async_computation.14 | async-start | bytes 3538944 | tf_op jit(solution)/shard_map/psum | solution.py:23
  348.8 5.8 copy-start.62
  356.8 3.0 copy-start.55
  356.8 3.0 copy-start.58
  359.5 176.3 %all-reduce.14.cloned.1.call-start = ((), (), s32[]{:S(2)}) async-start(), calls=%async_computation.15 | async-start | bytes 3538944 | tf_op jit(solution)/shard_map/psum | solution.py:23
  435.2 3.3 copy-start.12
  439.1 4.7 copy-start.52
  447.5 4.6 copy-start.20
  447.5 4.6 slice-start
  447.5 4.6 slice-start.1
  461.1 135.5 %all-reduce.16.cloned.1.call-start = ((), (), s32[]{:S(2)}) async-start(), calls=%async_computation.16 | async-start | bytes 2949120 | tf_op jit(solution)/shard_map/psum | solution.py:278
  461.2 2.7 copy-start.21
  469.2 3.1 copy-start.19
  469.2 165.4 %reduce-scatter.16.cloned.1.call-start = ((), (), s32[]{:S(2)}) async-start(), calls=%async_computation.21 | async-start | bytes 995328 | tf_op jit(solution)/shard_map/reduce_scatter | solution.py:315
  472.2 63.6 %copy-start.53 = (f32[16,17]{1,0:T(8,128)S(1)}, f32[16,17]{1,0:T(8,128)}, u32[]{:S(2)}) copy-start(f32[16,17]{1,0:T(8,128)} %copy-done.52) | copy-start | bytes 3268
  472.2 200.7 %reduce-scatter.14.cloned.1.call-start = ((), (), s32[]{:S(2)}) async-start(), calls=%async_computation.20 | async-start | bytes 995328 | tf_op jit(solution)/shard_map/reduce_scatter | solution.py:312
  475.9 65.0 %copy-start.32 = (f32[16,1152]{1,0:T(8,128)S(1)}, f32[16,1152]{1,0:T(8,128)}, u32[]{:S(2)}) copy-start(f32[16,1152]{1,0:T(8,128)} %copy-done.31) | copy-start | bytes 221188
  476.0 236.2 %reduce-scatter.12.cloned.1.call-start = ((), (), s32[]{:S(2)}) async-start(), calls=%async_computation.19 | async-start | bytes 995328 | tf_op jit(solution)/shard_map/reduce_scatter | solution.py:309
  540.9 3.3 copy-start.34
  547.0 212.3 %reduce-scatter.18.cloned.1.call-start = ((), (), s32[]{:S(2)}) async-start(), calls=%async_computation.22 | async-start | bytes 2985984 | tf_op jit(solution)/shard_map/reduce_scatter | solution.py:318
  551.9 254.9 %reduce-scatter.20.cloned.1.call-start = ((), (), s32[]{:S(2)}) async-start(), calls=%async_computation.23 | async-start | bytes 2985984 | tf_op jit(solution)/shard_map/reduce_scatter | solution.py:321
  556.7 387.1 %all-reduce.18.cloned.1.call-start = ((), (), s32[]{:S(2)}) async-start(), calls=%async_computation.24 | async-start | bytes 7077888 | tf_op jit(solution)/shard_map/psum | solution.py:23
  564.0 2.8 copy-start.44
  568.8 1.8 copy-start.16
  581.9 417.3 %reduce-scatter.10.cloned.1.call-start = ((), (), s32[]{:S(2)}) async-start(), calls=%async_computation.18 | async-start | bytes 2985984 | tf_op jit(solution)/shard_map/reduce_scatter | solution.py:306
  591.9 466.9 %reduce-scatter.8.cloned.1.call-start = ((), (), s32[]{:S(2)}) async-start(), calls=%async_computation.17 | async-start | bytes 4423680 | tf_op jit(solution)/shard_map/reduce_scatter | solution.py:302
  611.1 332.8 %copy-start.23 = (f32[16,1152]{1,0:T(8,128)S(1)}, f32[16,1152]{1,0:T(8,128)}, u32[]{:S(2)}) copy-start(f32[16,1152]{1,0:T(8,128)} %copy-done.22) | copy-start | bytes 221188
  761.2 184.8 %copy-start.51 = (f32[16,17]{1,0:T(8,128)S(1)}, f32[16,17]{1,0:T(8,128)}, u32[]{:S(2)}) copy-start(f32[16,17]{1,0:T(8,128)} %copy-done.50) | copy-start | bytes 3268
  943.9 2.1 copy-start.5
  947.5 1.6 copy-start.24
  947.5 1.6 copy-start.37
  949.9 26.2 %copy-start.49 = (f32[4,1152]{1,0:T(4,128)S(1)}, f32[4,1152]{1,0:T(4,128)}, u32[]{:S(2)}) copy-start(f32[4,1152]{1,0:T(4,128)} %param.18) | copy-start | bytes 55300
  (20 other events, 21.3 us)
Sparse Core Ops, SparseCore 0:
  10.0 37.6 all-gather.8
  49.5 36.4 all-gather.6
  87.9 26.5 all-gather.10
  122.0 75.7 all-reduce.7
  211.0 74.5 all-reduce.9
  287.3 29.2 all-gather.14
  318.5 30.2 all-gather.12
  359.6 75.5 all-reduce.11
  461.2 74.5 all-reduce.13
  538.9 57.6 all-reduce.15
  600.2 34.3 reduce-scatter.15
  637.7 35.1 reduce-scatter.13
  677.0 35.0 reduce-scatter.11
  715.5 43.7 reduce-scatter.17
  763.0 43.7 reduce-scatter.19
  809.7 134.1 all-reduce.17
  947.2 42.9 reduce-scatter.9
  992.4 66.3 reduce-scatter.7
where the time goes:
time: 1080 us; the launch traced here: 1070 us
  waiting for transfers between devices  733 us (68%)
  matrix products  105 us (10%)
  blocking collectives  95.8 us (9%)
  local copies, waits for them, and re-layouts  71.9 us (7%)
  other arithmetic  45.7 us (4%)
  between operations  15.4 us (1%)
    psum x5, waiting for transfers between devices, total_rows(): return lax.psum(partial_value, 'tp')  407 us
    reduce_scatter x1, waiting for transfers between devices, shards(): lax.psum_scatter(caption_part.astype(jnp.bfloat16), 'tp', scatter_dimensi...  57.7 us
    reduce_scatter x1, waiting for transfers between devices, shards(): lax.psum_scatter(grad_down.astype(jnp.bfloat16), 'seq', scatter_dimension...  45.7 us
    reduce_scatter x1, waiting for transfers between devices, shards(): lax.psum_scatter(grad_up.astype(jnp.bfloat16), 'seq', scatter_dimension=0...  45.6 us
    reduce_scatter x1, waiting for transfers between devices, shards(): lax.psum_scatter(grad_out.astype(jnp.bfloat16), 'seq', scatter_dimension=...  37.7 us
    reduce_scatter x1, waiting for transfers between devices, shards(): lax.psum_scatter(grad_query2.astype(jnp.bfloat16), 'seq', scatter_dimensi...  36.7 us
    all_gather x1, waiting for transfers between devices, shards(): lax.all_gather(w_up, 'seq', axis=0, tiled=True)  28.1 us
    psum x1, blocking collectives, shards(): lax.psum(d_mods.astype(jnp.bfloat16), 'seq').astype(jnp.float32)  24.9 us
  transfers between devices with their start and end apart: 18, of which 15 were waited for; matrix products, arithmetic and copies ran while one was open for 15% of the time, Pallas kernels for 0%

commit v1 on v0

--- a/solution.py
+++ b/solution.py
@@ -10,6 +10,11 @@
 HIGHEST = lax.Precision.HIGHEST
 
 
+def add_all(x, mesh_axis):
+    parts = lax.all_gather(x, mesh_axis)
+    return jnp.sum(parts, axis=0)
+
+
 def normalize(rows):
     center = rows - jnp.mean(rows, -1, keepdims=True)
     return center * lax.rsqrt(jnp.mean(center * center, -1, keepdims=True) + EPSILON)
@@ -20,7 +25,7 @@
 
 
 def total_rows(partial_value):
-    return lax.psum(partial_value, "tp")
+    return add_all(partial_value, "tp")
 
 
 def frame_attention(triple, live, head_scale):

time: 1080 us -> 1260 us (1.17)
  waiting for transfers between devices: 733 us -> 902 us
  other arithmetic: 45.7 us -> 71 us
    all_gather x0 -> x6, waiting for transfers between devices: none -> 504 us  [add_all(): parts = lax.all_gather(x, mesh_axis)]
    psum x5 -> x0, waiting for transfers between devices: 407 us -> none  [total_rows(): return lax.psum(partial_value, 'tp')]
    reduce_scatter x1, waiting for transfers between devices: 0.01 us -> 45.5 us  [shards(): lax.psum_scatter(grad_qkv.astype(jnp.bfloat16), 'seq', scatter_dimension=...]
    reduce_scatter x1, waiting for transfers between devices: 45.6 us -> 13.3 us  [shards(): lax.psum_scatter(grad_up.astype(jnp.bfloat16), 'seq', scatter_dimension=0...]
    psum x1, waiting for transfers between devices: 4.67 us -> 21.5 us  [shards(): lax.psum(kv_grad.astype(jnp.bfloat16), 'seq').astype(jnp.float32)]
    reduce_sum x1 -> x5, other arithmetic: 0.85 us -> 17.6 us  [add_all(): return jnp.sum(parts, axis=0)]
    all_gather x1, waiting for transfers between devices: 0.01 us -> 16.8 us  [shards(): lax.all_gather(w_qkv, 'seq', axis=0, tiled=True)]
    all_gather x1, waiting for transfers between devices: 21.8 us -> 35.3 us  [shards(): lax.all_gather(w_ada, 'seq', axis=0, tiled=True)]
  transfers between devices with their start and end apart: 18 -> 19, of which waited for: 15 -> 18; matrix products, arithmetic and copies ran while one was open for 15% -> 13% of each run, Pallas kernels for 0% -> 0%
where the time goes in v1:
time: 1260 us
  waiting for transfers between devices  902 us (72%)
  matrix products  96.7 us (8%)
  blocking collectives  92.3 us (7%)
  local copies, waits for them, and re-layouts  75.5 us (6%)
  other arithmetic  71 us (6%)
  between operations  15.5 us (1%)
    all_gather x6, waiting for transfers between devices, add_all(): parts = lax.all_gather(x, mesh_axis)  504 us
    reduce_scatter x1, waiting for transfers between devices, shards(): lax.psum_scatter(caption_part.astype(jnp.bfloat16), 'tp', scatter_dimensi...  67.1 us
    reduce_scatter x1, waiting for transfers between devices, shards(): lax.psum_scatter(grad_qkv.astype(jnp.bfloat16), 'seq', scatter_dimension=...  45.5 us
    reduce_scatter x1, waiting for transfers between devices, shards(): lax.psum_scatter(grad_down.astype(jnp.bfloat16), 'seq', scatter_dimension...  45.4 us
    reduce_scatter x1, waiting for transfers between devices, shards(): lax.psum_scatter(grad_query2.astype(jnp.bfloat16), 'seq', scatter_dimensi...  36.6 us
    reduce_scatter x1, waiting for transfers between devices, shards(): lax.psum_scatter(grad_out.astype(jnp.bfloat16), 'seq', scatter_dimension=...  35.5 us
    all_gather x1, waiting for transfers between devices, shards(): lax.all_gather(w_ada, 'seq', axis=0, tiled=True)  35.3 us
    reduce_scatter x1, waiting for transfers between devices, shards(): lax.psum_scatter(grad_out2.astype(jnp.bfloat16), 'seq', scatter_dimension...  33.5 us
  transfers between devices with their start and end apart: 19, of which 18 were waited for; matrix products, arithmetic and copies ran while one was open for 13% of the time, Pallas kernels for 0%

profile of v1, /device:TPU:0, one launch (start us, length us, event | category | flops | bytes accessed | tf_op | source)
XLA Modules:
  0.0 1255.1 jit_solution(18203681360899884402)
XLA Ops:
  13.3 14.3 %all_gather.48 = bf16[288,1152]{0,1:T(8,128)(2,1)S(1)} all-gather(bf16[288,144]{0,1:T(8,128)(2,1)S(1)} %copy-done.49), channel_id=1, replica_groups=mesh['seq'=8,'tp'=4] {'seq'}, dimensions={1}, use_global_device_ids=true | all-gather | bytes 746496 | tf_op jit(solution)/shard_map/all_gather | solution.py:78
  27.6 16.8 %all-gather.19.cloned.1.call-done = bf16[1152,3,288]{2,0,1:T(8,128)(2,1)} async-done(((bf16[144,3,288]{2,0,1:T(8,128)(2,1)}), bf16[1152,3,288]{2,0,1:T(8,128)(2,1)}) %all-gather.19.cloned.1.call-update) | async-done | bytes 1990672 | tf_op jit(solution)/shard_map/all_gather | solution.py:77
  44.4 3.0 copy.168
  47.4 35.3 %all-gather.17.cloned.1.call-done = bf16[1152,1728]{1,0:T(8,128)(2,1)} async-done(((bf16[144,1728]{1,0:T(8,128)(2,1)}), bf16[1152,1728]{1,0:T(8,128)(2,1)}) %all-gather.17.cloned.1.call-update) | async-done | bytes 3981328 | tf_op jit(solution)/shard_map/all_gather | solution.py:84
  82.7 2.8 convolution_bitcast_fusion
  85.6 13.4 %all-gather.4 = f32[4,1728,4]{1,2,0:T(4,128)S(1)} all-gather(f32[1,1728,4]{1,2,0:T(4,128)S(1)} %convolution_bitcast_fusion), channel_id=1, replica_groups=mesh['seq'=8,'tp'=4] {'tp'}, dimensions={0}, use_global_device_ids=true | all-gather | bytes 138240 | tf_op jit(solution)/shard_map/all_gather | solution.py:90
  106.7 2.2 reshape.353
  109.0 2.8 convolution_convert_fusion.9
  111.8 2.3 reshape.355
  124.4 10.6 all_gather.51
  135.0 12.4 all_gather.52
  147.8 6.5 copy.178
  154.4 5.4 convolution_convert_fusion.4
  159.8 54.6 %all-gather.31.cloned.1.call-done = f32[64,17,1152]{2,0,1:T(8,128)} async-done(((f32[16,17,1152]{2,0,1:T(8,128)}), f32[64,17,1152]{2,0,1:T(8,128)}) %all-gather.31.cloned.1.call-update) | async-done | bytes 5013520 | tf_op jit(solution)/shard_map/all_gather | solution.py:14
  214.4 2.9 reduce_sum.249
  218.8 2.2 reshape.360
  221.0 2.3 convolution_convert_fusion.13
  224.5 2.6 fusion.107
  234.7 91.4 %all-gather.33.cloned.1.call-done = f32[64,17,1152]{2,0,1:T(8,128)} async-done(((f32[16,17,1152]{2,0,1:T(8,128)}), f32[64,17,1152]{2,0,1:T(8,128)}) %all-gather.33.cloned.1.call-update) | async-done | bytes 5013520 | tf_op jit(solution)/shard_map/all_gather | solution.py:14
  326.1 3.9 reduce_sum.255
  330.1 2.8 fusion.104
  335.9 2.2 reshape.363
  340.4 16.2 %all-gather.25.cloned.1.call-done = bf16[1152,1152]{0,1:T(8,128)(2,1)} async-done(((bf16[1152,144]{0,1:T(8,128)(2,1)}), bf16[1152,1152]{0,1:T(8,128)(2,1)}) %all-gather.25.cloned.1.call-update) | async-done | bytes 2654224 | tf_op jit(solution)/shard_map/all_gather | solution.py:83
  356.5 4.1 fusion.108
  360.6 28.1 %all-gather.23.cloned.1.call-done = bf16[1152,1152]{1,0:T(8,128)(2,1)} async-done(((bf16[144,1152]{1,0:T(8,128)(2,1)}), bf16[1152,1152]{1,0:T(8,128)(2,1)}) %all-gather.23.cloned.1.call-update) | async-done | bytes 2654224 | tf_op jit(solution)/shard_map/all_gather | solution.py:82
  388.7 5.0 fusion.47
  396.7 2.7 all_gather_reshape.5
  399.4 2.8 copy.186
  403.9 92.7 %all-gather.29.cloned.1.call-done = f32[4,16,17,1152]{3,1,2,0:T(8,128)} async-done(((f32[1,16,17,1152]{3,1,2,0:T(8,128)}), f32[4,16,17,1152]{3,1,2,0:T(8,128)}) %all-gather.29.cloned.1.call-update) | async-done | bytes 5013520 | tf_op jit(solution)/shard_map/all_gather | solution.py:14
  496.6 3.7 fusion.103
  507.4 2.6 convolution_convert_fusion.12
  511.7 3.9 fusion.16
  515.6 4.3 multiply_reduce_fusion
  524.2 4.5 fusion.101
  528.7 2.7 all_gather_reshape.4
  531.3 2.8 copy.183
  534.2 3.7 fusion.49
  541.8 2.6 fusion.52
  544.6 4.5 convolution_convert_fusion.1
  550.2 4.6 convolution_convert_fusion
  554.9 3.0 convolution_convert_fusion.5
  559.7 21.5 %all-reduce.2.cloned.1.call-done = bf16[1200,2,4,72]{0,3,2,1:T(8,128)(2,1)} async-done(((bf16[1200,2,4,72]{0,3,2,1:T(8,128)(2,1)}), bf16[1200,2,4,72]{0,3,2,1:T(8,128)(2,1)}) %all-reduce.2.cloned.1.call-update) | async-done | bytes 1382416 | tf_op jit(solution)/shard_map/psum | solution.py:283
  581.3 4.2 dot_general.167
  585.5 6.6 convolution_convert_fusion.2
  595.7 80.7 %all-gather.27.cloned.1.call-done = f32[4,16,17,1152]{3,1,2,0:T(8,128)} async-done(((f32[1,16,17,1152]{3,1,2,0:T(8,128)}), f32[4,16,17,1152]{3,1,2,0:T(8,128)}) %all-gather.27.cloned.1.call-update) | async-done | bytes 5013520 | tf_op jit(solution)/shard_map/all_gather | solution.py:14
  676.4 3.9 reduce_sum.261
  680.3 90.4 %all-gather.35.cloned.1.call-done = f32[64,17,1152]{2,0,1:T(8,128)} async-done(((f32[16,17,1152]{2,0,1:T(8,128)}), f32[64,17,1152]{2,0,1:T(8,128)}) %all-gather.35.cloned.1.call-update) | async-done | bytes 5013520 | tf_op jit(solution)/shard_map/all_gather | solution.py:14
  770.8 4.0 reduce_sum.269
  774.7 6.1 fusion.25
  793.4 4.4 convolution_convert_fusion.3
  803.4 13.3 %reduce-scatter.18.cloned.1.call-done = bf16[144,1152]{1,0:T(8,128)(2,1)} async-done(((bf16[1152,1152]{1,0:T(8,128)(2,1)}), bf16[144,1152]{1,0:T(8,128)(2,1)}) %reduce-scatter.18.cloned.1.call-update) | async-done | bytes 331792 | tf_op jit(solution)/shard_map/reduce_scatter | solution.py:323
  818.5 45.4 %reduce-scatter.20.cloned.1.call-done = bf16[1152,144]{0,1:T(8,128)(2,1)} async-done(((bf16[1152,1152]{0,1:T(8,128)(2,1)}), bf16[1152,144]{0,1:T(8,128)(2,1)}) %reduce-scatter.20.cloned.1.call-update) | async-done | bytes 331792 | tf_op jit(solution)/shard_map/reduce_scatter | solution.py:326
  868.9 33.5 %reduce-scatter.16.cloned.1.call-done = bf16[288,144]{0,1:T(8,128)(2,1)} async-done(((bf16[288,1152]{0,1:T(8,128)(2,1)}), bf16[288,144]{0,1:T(8,128)(2,1)}) %reduce-scatter.16.cloned.1.call-update) | async-done | bytes 82960 | tf_op jit(solution)/shard_map/reduce_scatter | solution.py:320
  904.1 36.6 %reduce-scatter.14.cloned.1.call-done = bf16[144,288]{1,0:T(8,128)(2,1)} async-done(((bf16[1152,288]{1,0:T(8,128)(2,1)}), bf16[144,288]{1,0:T(8,128)(2,1)}) %reduce-scatter.14.cloned.1.call-update) | async-done | bytes 82960 | tf_op jit(solution)/shard_map/reduce_scatter | solution.py:317
  942.3 67.1 %reduce-scatter.8.cloned.1.call-done = bf16[4,300,288]{1,2,0:T(8,128)(2,1)} async-done(((bf16[4,300,1152]{1,2,0:T(8,128)(2,1)}), bf16[4,300,288]{1,2,0:T(8,128)(2,1)}) %reduce-scatter.8.cloned.1.call-update) | async-done | bytes 691216 | tf_op jit(solution)/shard_map/reduce_scatter | solution.py:307
  1009.4 2.5 convert_element_type.205
  1012.7 35.5 %reduce-scatter.12.cloned.1.call-done = bf16[288,144]{0,1:T(8,128)(2,1)} async-done(((bf16[288,1152]{0,1:T(8,128)(2,1)}), bf16[288,144]{0,1:T(8,128)(2,1)}) %reduce-scatter.12.cloned.1.call-update) | async-done | bytes 82960 | tf_op jit(solution)/shard_map/reduce_scatter | solution.py:314
  1049.8 45.5 %reduce-scatter.10.cloned.1.call-done = bf16[144,3,288]{2,0,1:T(8,128)(2,1)} async-done(((bf16[1152,3,288]{2,0,1:T(8,128)(2,1)}), bf16[144,3,288]{2,0,1:T(8,128)(2,1)}) %reduce-scatter.10.cloned.1.call-update) | async-done | bytes 248848 | tf_op jit(solution)/shard_map/reduce_scatter | solution.py:311
  1097.2 94.1 %all-gather.37.cloned.1.call-done = f32[64,17,1152]{2,0,1:T(8,128)} async-done(((f32[16,17,1152]{2,0,1:T(8,128)}), f32[64,17,1152]{2,0,1:T(8,128)}) %all-gather.37.cloned.1.call-update) | async-done | bytes 5013520 | tf_op jit(solution)/shard_map/all_gather | solution.py:14
  1191.3 2.9 reduce_sum.274
  1194.2 2.7 reduce.2
  1201.1 24.6 %psum.22 = bf16[4,6912]{1,0:T(4,128)(2,1)S(1)} all-reduce(bf16[4,6912]{1,0:T(4,128)(2,1)S(1)} %bitcast.210), channel_id=1, replica_groups=mesh['seq'=8,'tp'=4] {'seq'}, use_global_device_ids=true, to_apply=%region_31.32 | all-reduce | flops 27648 | bytes 110592 | tf_op jit(solution)/shard_map/psum | solution.py:284
  1227.8 3.4 fusion.78
  1231.1 17.0 %psum.23 = f32[4,1152]{1,0:T(4,128)} all-reduce(f32[4,1152]{1,0:T(4,128)S(1)} %fusion.78), channel_id=1, replica_groups=mesh['seq'=8,'tp'=4] {'tp'}, use_global_device_ids=true, to_apply=%region_32.33 | all-reduce | flops 4608 | bytes 36864 | tf_op jit(solution)/shard_map/psum | solution.py:296
  (279 shorter events, 106.5 us)
Async XLA Ops:
  7.2 5.0 copy-start.1
  7.2 5.4 copy-start.51
  7.2 6.1 copy-start.49
  7.2 37.2 %all-gather.19.cloned.1.call-start = ((), (), s32[]{:S(2)}) async-start(), calls=%async_computation.8 | async-start | bytes 2985984 | tf_op jit(solution)/shard_map/all_gather | solution.py:77
  7.9 74.8 %all-gather.17.cloned.1.call-start = ((), (), s32[]{:S(2)}) async-start(), calls=%async_computation.7 | async-start | bytes 4644864 | tf_op jit(solution)/shard_map/all_gather | solution.py:84
  8.7 139.1 %all-gather.21.cloned.1.call-start = ((), (), s32[]{:S(2)}) async-start(), calls=%async_computation.9 | async-start | bytes 1990656 | tf_op jit(solution)/shard_map/all_gather | solution.py:80
  9.4 205.0 %all-gather.31.cloned.1.call-start = ((), (), s32[]{:S(2)}) async-start(), calls=%async_computation.22 | async-start | bytes 6266880 | tf_op jit(solution)/shard_map/all_gather | solution.py:14
  12.6 34.8 %copy-start.53 = (f32[16,17]{1,0:T(8,128)}, f32[16,17]{1,0:T(8,128)S(1)}, u32[]{:S(2)}) copy-start(f32[16,17]{1,0:T(8,128)S(1)} %fusion.34) | copy-start | bytes 3268
  27.6 90.8 %copy-start.9 = (bf16[288,1152]{0,1:T(8,128)(2,1)}, bf16[288,1152]{0,1:T(8,128)(2,1)S(1)}, u32[]{:S(2)}) copy-start(bf16[288,1152]{0,1:T(8,128)(2,1)S(1)} %all_gather.48) | copy-start | bytes 1990660
  47.4 61.6 %copy-start.7 = (bf16[1152,3,288]{0,2,1:T(8,128)(2,1)}, bf16[1152,3,288]{0,2,1:T(8,128)(2,1)S(1)}, u32[]{:S(2)}) copy-start(bf16[1152,3,288]{0,2,1:T(8,128)(2,1)S(1)} %copy.168) | copy-start | bytes 5971972
  115.0 3.0 copy-start.29
  115.0 3.0 copy-start.31
  118.1 2.0 copy-start.33
  118.4 1.7 copy-start.62
  120.1 206.1 %all-gather.33.cloned.1.call-start = ((), (), s32[]{:S(2)}) async-start(), calls=%async_computation.23 | async-start | bytes 6266880 | tf_op jit(solution)/shard_map/all_gather | solution.py:14
  122.4 1.9 copy-start.63
  214.4 2.9 copy-start.34
  217.4 3.7 copy-start.4
  224.4 2.6 copy-start.23
  227.1 2.4 copy-start
  227.1 2.4 copy-start.59
  227.1 2.5 copy-start.19
  229.6 2.1 copy-start.12
  231.1 2.2 copy-start.35
  233.3 123.2 %all-gather.25.cloned.1.call-start = ((), (), s32[]{:S(2)}) async-start(), calls=%async_computation.11 | async-start | bytes 2985984 | tf_op jit(solution)/shard_map/all_gather | solution.py:83
  233.9 154.8 %all-gather.23.cloned.1.call-start = ((), (), s32[]{:S(2)}) async-start(), calls=%async_computation.10 | async-start | bytes 2985984 | tf_op jit(solution)/shard_map/all_gather | solution.py:82
  234.7 261.9 %all-gather.29.cloned.1.call-start = ((), (), s32[]{:S(2)}) async-start(), calls=%async_computation.13 | async-start | bytes 6266880 | tf_op jit(solution)/shard_map/all_gather | solution.py:14
  333.2 2.7 copy-start.55
  388.7 5.8 copy-start.64
  399.4 3.3 copy-start.60
  402.2 179.1 %all-reduce.2.cloned.1.call-start = ((), (), s32[]{:S(2)}) async-start(), calls=%async_computation.14 | async-start | bytes 2949120 | tf_op jit(solution)/shard_map/psum | solution.py:283
  500.3 2.4 copy-start.2
  501.0 2.3 copy-start.15
  511.7 3.9 copy-start.20
  511.7 3.9 copy-start.26
  511.7 3.9 copy-start.50
  511.7 8.2 slice-start
  515.6 4.3 slice-start.1
  521.3 1.6 copy-start.3
  524.2 152.2 %all-gather.27.cloned.1.call-start = ((), (), s32[]{:S(2)}) async-start(), calls=%async_computation.12 | async-start | bytes 6266880 | tf_op jit(solution)/shard_map/all_gather | solution.py:14
  534.1 236.6 %all-gather.35.cloned.1.call-start = ((), (), s32[]{:S(2)}) async-start(), calls=%async_computation.24 | async-start | bytes 6266880 | tf_op jit(solution)/shard_map/all_gather | solution.py:14
  544.4 272.3 %reduce-scatter.18.cloned.1.call-start = ((), (), s32[]{:S(2)}) async-start(), calls=%async_computation.20 | async-start | bytes 2985984 | tf_op jit(solution)/shard_map/reduce_scatter | solution.py:323
  549.2 314.8 %reduce-scatter.20.cloned.1.call-start = ((), (), s32[]{:S(2)}) async-start(), calls=%async_computation.21 | async-start | bytes 2985984 | tf_op jit(solution)/shard_map/reduce_scatter | solution.py:326
  554.8 3.1 copy-start.17
  554.8 3.1 copy-start.25
  554.8 347.6 %reduce-scatter.16.cloned.1.call-start = ((), (), s32[]{:S(2)}) async-start(), calls=%async_computation.19 | async-start | bytes 995328 | tf_op jit(solution)/shard_map/reduce_scatter | solution.py:320
  557.9 382.8 %reduce-scatter.14.cloned.1.call-start = ((), (), s32[]{:S(2)}) async-start(), calls=%async_computation.18 | async-start | bytes 995328 | tf_op jit(solution)/shard_map/reduce_scatter | solution.py:317
  559.7 449.7 %reduce-scatter.8.cloned.1.call-start = ((), (), s32[]{:S(2)}) async-start(), calls=%async_computation.15 | async-start | bytes 4423680 | tf_op jit(solution)/shard_map/reduce_scatter | solution.py:307
  592.1 456.1 %reduce-scatter.12.cloned.1.call-start = ((), (), s32[]{:S(2)}) async-start(), calls=%async_computation.17 | async-start | bytes 995328 | tf_op jit(solution)/shard_map/reduce_scatter | solution.py:314
  770.7 4.0 copy-start.16
  770.8 4.0 copy-start.58
  782.2 1.9 copy-start.47
  784.0 1.8 copy-start.44
  787.1 2.2 copy-start.45
  787.2 2.2 copy-start.48
  789.2 2.0 copy-start.30
  789.3 306.1 %reduce-scatter.10.cloned.1.call-start = ((), (), s32[]{:S(2)}) async-start(), calls=%async_computation.16 | async-start | bytes 2985984 | tf_op jit(solution)/shard_map/reduce_scatter | solution.py:311
  797.9 3.5 copy-start.8
  797.9 393.4 %all-gather.37.cloned.1.call-start = ((), (), s32[]{:S(2)}) async-start(), calls=%async_computation.25 | async-start | bytes 6266880 | tf_op jit(solution)/shard_map/all_gather | solution.py:14
  803.3 62.4 %copy-start.13 = (bf16[1200,2,4,72]{0,3,2,1:T(8,128)(2,1)S(1)}, bf16[1200,2,4,72]{0,3,2,1:T(8,128)(2,1)}, u32[]{:S(2)}) copy-start(bf16[1200,2,4,72]{0,3,2,1:T(8,128)(2,1)} %all-reduce.2.cloned.1.call-done) | copy-start | bytes 4147204
  868.9 142.9 %copy-start.18 = (bf16[16,17,1152]{2,1,0:T(8,128)(2,1)S(1)}, bf16[16,17,1152]{2,1,0:T(8,128)(2,1)}, u32[]{:S(2)}) copy-start(bf16[16,17,1152]{2,1,0:T(8,128)(2,1)} %get-tuple-element.145) | copy-start | bytes 1880068
  1194.2 2.8 copy-start.28
  1197.0 1.9 copy-start.6
  1199.8 28.0 %copy-start.52 = (f32[4,1152]{1,0:T(4,128)S(1)}, f32[4,1152]{1,0:T(4,128)}, u32[]{:S(2)}) copy-start(f32[4,1152]{1,0:T(4,128)} %param.18) | copy-start | bytes 55300
  (23 other events, 24.4 us)
Sparse Core Ops, SparseCore 0:
  9.9 34.3 all-gather.18
  46.3 36.4 all-gather.16
  84.6 26.5 all-gather.20
  120.2 94.2 all-gather.30
  233.5 92.6 all-gather.32
  327.9 28.6 all-gather.24
  358.4 30.2 all-gather.22
  402.3 94.2 all-gather.28
  524.3 56.9 all-reduce.1
  582.8 93.5 all-gather.26
  678.0 92.6 all-gather.34
  774.5 42.1 reduce-scatter.17
  820.1 43.7 reduce-scatter.19
  867.3 35.0 reduce-scatter.15
  905.5 35.0 reduce-scatter.13
  943.0 66.3 reduce-scatter.7
  1012.8 35.4 reduce-scatter.11
  1051.6 43.7 reduce-scatter.9
  1097.0 94.2 all-gather.36
